TPU v7x, 256 devices: a whole 4x4x8 slice. The times are simulated.
256 devices in a mesh: exp: 64 (over z, x, core), sub: 4 (over y).
Axes of the slice: x: 4, y: 4, z: 8, core: 2. Of those that a mesh axis runs over, the one named last changes fastest.
Arguments:
- sky_map: float32 [256, 8, 8, 128], P(('exp', 'sub')), may hold values from -6 to 6
- coeffs: bfloat16 [128, 12, 512, 512], P('exp', None, 'sub'), may hold values from -1.75 to 1.75
- observed: float32 [128, 512, 512], P('exp', 'sub'), may hold values from -6 to 6
- vert_taps: bfloat16 [12, 21], replicated, may hold values from -1.25 to 1.25
- horiz_taps: bfloat16 [12, 21], replicated, may hold values from -1.25 to 1.25
- owner_ids: int32 [128, 64, 4, 1], P('exp', 'sub'), may hold values from 0 to 63; in each aligned block of 64 rows (0 to 63, 64 to 127, ..., all dimensions but the last counted through in order) at most 2 rows name the same one
- offset: int32 [128, 64, 4], P('exp', 'sub'), may hold values from 0 to 7
Outputs:
- sky_final: float32 [256, 8, 8, 128], P(('exp', 'sub'))
- clipped: float32 [128, 512, 512], P('exp', 'sub')
Inputs may be any that keep to these rules, and one draw needn't show every extreme that they name: Patch (e, r, q) reads sky tile owner_ids[e, r, q, 0] * 4 + r // 16. Among the 64 patches of one band of one piece (the rows of one device's piece) no owner is named more than 2 times, and in every draw some band names one owner exactly 2 times.
All inputs are finite; a program needn't handle non-finite values.
Results may differ from a plain program's by a relative error of at most 0.0035.
Values may be sent and summed in bfloat16 or wider, within the bound.
A program may use at most 64 MiB of HBM per device.

v0:
```python
import jax
import jax.numpy as jnp
from jax import lax
from jax.sharding import PartitionSpec as P

STEPS = 2
ETA = 0.5
DELTA = 1.0


def padded_2(cells, sides, width):
    for axis, dim in sides:
        count = lax.axis_size(axis)
        ends = count - 1
        head = lax.slice_in_dim(cells, 0, width, axis=dim)
        tail = lax.slice_in_dim(cells, cells.shape[dim] - width, cells.shape[dim], axis=dim)
        cells = jnp.concatenate(
            [
                lax.ppermute(tail, axis, [(i, (i + 1) % count) for i in range(ends)]),
                cells,
                lax.ppermute(head, axis, [((i + 1) % count, i) for i in range(ends)]),
            ],
            axis=dim,
        )
    return cells


def from_behind(block, axis, distance):
    devices = range(lax.axis_size(axis))
    route = [(i - distance, i) for i in devices if i - distance in devices]
    return lax.ppermute(block, axis, route)


def band_table(filters, height, breadth, direction):
    row_ids = lax.broadcasted_iota(jnp.int32, (height, breadth), 0)
    col_ids = lax.broadcasted_iota(jnp.int32, (height, breadth), 1)
    lag_ids = direction * (col_ids - row_ids)
    tap_ids = lax.broadcasted_iota(jnp.int32, (filters.shape[1], height, breadth), 0)
    select = (tap_ids == lag_ids[None]).astype(jnp.float32)
    return jnp.einsum("mt,tij->mij", filters.astype(jnp.float32), select).astype(jnp.bfloat16)


def per_device(sky_map, coeffs, observed, vert_taps, horiz_taps, owner_ids, offset):
    pieces, height, breadth = observed.shape
    mode_count = coeffs.shape[1]
    per_tile = sky_map.shape[1]
    patch_rows = sky_map.shape[2]
    patch_cols = sky_map.shape[3]
    patch_size = patch_rows * patch_cols
    margin = (vert_taps.shape[1] - 1) // 2
    exp_count = lax.axis_size("exp")
    rows_band = height // patch_rows
    cols_band = breadth // patch_cols
    per_band = rows_band * cols_band
    requests = pieces * per_band
    vertical = band_table(vert_taps, height, height + 2 * margin, 1)
    horizontal = band_table(horiz_taps, patch_cols + 2 * margin, patch_cols, -1)
    owners = owner_ids.reshape(requests)
    offsets = offset.reshape(requests)
    all_ids = owners * per_tile + offsets
    table_f = (
        all_ids[:, None] == lax.broadcasted_iota(jnp.int32, (1, exp_count * per_tile), 1)
    ).astype(jnp.float32)
    table_b = table_f.astype(jnp.bfloat16)
    counts = lax.psum_scatter(
        jnp.sum(table_f, axis=0).reshape(exp_count, per_tile),
        "exp",
        scatter_dimension=0,
        tiled=True,
    ).reshape(per_tile)
    current = sky_map.reshape(per_tile, patch_size)
    clipped = jnp.zeros(observed.shape, jnp.float32)
    for step_index in range(STEPS):
        shard_piece = lax.all_gather(
            current.astype(jnp.bfloat16).reshape(1, per_tile, patch_size), "exp", axis=0, tiled=True
        )
        tile_count = shard_piece.shape[0]
        patches = jnp.dot(
            table_b,
            shard_piece.reshape(tile_count * per_tile, patch_size),
            preferred_element_type=jnp.float32,
        ).astype(jnp.bfloat16)
        to_stacked = patches.reshape(pieces, rows_band, cols_band, patch_rows, patch_cols)
        extended = padded_2(
            to_stacked.transpose(0, 1, 3, 2, 4).reshape(pieces, height, breadth),
            (("sub", 1),),
            margin,
        )
        smoothed = jnp.einsum(
            "mia,pac->pmic", vertical, extended, preferred_element_type=jnp.float32
        ).astype(jnp.bfloat16)
        padded = jnp.pad(smoothed, ((0, 0), (0, 0), (0, 0), (margin, margin)))
        windows = jnp.stack(
            [
                padded[
                    ...,
                    block_index * patch_cols : block_index * patch_cols + patch_cols + 2 * margin,
                ]
                for block_index in range(cols_band)
            ],
            axis=3,
        )
        blurred = jnp.einsum(
            "pmbkw,mwc->pmbkc", windows, horizontal, preferred_element_type=jnp.float32
        ).reshape(pieces, mode_count, height, breadth)
        modeled = jnp.sum(coeffs.astype(jnp.float32) * blurred, axis=1)
        evaluate_clipped = jnp.clip(modeled - observed, -DELTA, DELTA)
        weighted = (coeffs.astype(jnp.float32) * evaluate_clipped[:, None]).astype(jnp.bfloat16)
        spread = jnp.einsum(
            "pmbkc,mwc->pmbkw",
            weighted.reshape(pieces, mode_count, height, cols_band, patch_cols),
            horizontal,
            preferred_element_type=jnp.float32,
        )
        summed = jnp.zeros((pieces, mode_count, height, breadth + 2 * margin), jnp.float32)
        for block_index in range(cols_band):
            summed = summed + jnp.pad(
                spread[:, :, :, block_index],
                (
                    (0, 0),
                    (0, 0),
                    (0, 0),
                    (block_index * patch_cols, breadth - (block_index + 1) * patch_cols),
                ),
            )
        back_rows = summed[..., margin : margin + breadth].astype(jnp.bfloat16)
        gathered_rows = jnp.einsum(
            "mia,pmic->pac", vertical, back_rows, preferred_element_type=jnp.float32
        )
        upper_rim = gathered_rows[:, :margin]
        lower_rim = gathered_rows[:, height + margin :]
        from_below = from_behind(upper_rim, "sub", -1)
        from_above = from_behind(lower_rim, "sub", 1)
        gradient = gathered_rows[:, margin : margin + height]
        gradient = (
            gradient
            + jnp.pad(from_above, ((0, 0), (0, height - margin), (0, 0)))
            + jnp.pad(from_below, ((0, 0), (height - margin, 0), (0, 0)))
        )
        clipped, gradient = (evaluate_clipped, gradient)
        stacked = gradient.reshape(pieces, rows_band, patch_rows, cols_band, patch_cols)
        grad_patches = stacked.transpose(0, 1, 3, 2, 4).reshape(requests, patch_size)
        summed = lax.psum_scatter(
            lax.dot_general(
                table_f, grad_patches, (((0,), (0,)), ((), ())), precision=lax.Precision.HIGHEST
            ),
            "exp",
            scatter_dimension=0,
            tiled=True,
        )
        current = current - ETA * summed / jnp.maximum(counts, 1.0)[:, None]
    return (current.reshape(sky_map.shape), clipped)


def solution(mesh):
    return jax.shard_map(
        per_device,
        mesh=mesh,
        in_specs=(
            P(("exp", "sub"), None, None, None),
            P("exp", None, "sub", None),
            P("exp", "sub", None),
            P(),
            P(),
            P("exp", "sub", None, None),
            P("exp", "sub", None),
        ),
        out_specs=(P(("exp", "sub"), None, None, None), P("exp", "sub", None)),
        check_vma=False,
    )
```

profile of v0, /device:TPU:8, one launch (start us, length us, event | category | flops | bytes accessed | tf_op | source)
XLA Modules:
  0.0 716.3 jit_solution(18267638803737350568)
XLA Ops:
  7.2 0.8 convert_element_type.96
  8.0 0.6 convert_element_type.97
  8.7 0.7 broadcast_multiply_fusion
  9.4 0.1 copy.84
  9.5 0.1 mul.53
  9.6 0.8 copy.85
  10.3 0.1 reshape.112
  10.5 0.5 fusion.26
  11.0 80.0 %all-gather.4.cloned.1.call-done = bf16[64,8,1024]{2,1,0:T(8,128)(2,1)} async-done(((bf16[1,8,1024]{2,1,0:T(8,128)(2,1)}), bf16[64,8,1024]{2,1,0:T(8,128)(2,1)}) %all-gather.4.cloned.1.call-update) | async-done | bytes 1048592 | tf_op jit(solution)/shard_map/all_gather | solution.py:74
  91.0 1.6 fusion.35
  92.7 3.4 collective-permute-start
  96.1 2.4 collective-permute-start.1
  98.5 1.2 fusion.34
  99.7 2.2 collective-permute-done.1
  101.9 1.0 convert_bitcast_fusion.1
  102.9 1.9 fusion.38
  104.8 3.3 fusion.8
  108.2 6.7 copy.89
  114.9 4.1 fusion
  119.0 0.1 subtract_clamp_fusion.1
  119.1 2.4 fusion.1
  121.6 5.5 reshape.117
  127.1 4.3 fusion.18
  131.4 0.6 slice_bitcast_fusion.7
  132.0 0.4 copy-done.6
  132.5 1.2 fusion.31
  133.7 3.1 collective-permute-start.2
  136.8 2.9 collective-permute-start.3
  139.7 0.1 collective-permute-done.2
  139.9 3.1 collective-permute-done.3
  143.0 2.4 fusion.47
  145.6 0.1 convert_reduce_fusion
  145.7 0.1 reshape.120
  145.8 0.6 dynamic-slice
  147.0 246.5 %all-reduce.15 = f32[64,8]{1,0:T(8,128)S(1)} all-reduce(f32[64,8]{1,0:T(8,128)S(1)} %reshape.120), channel_id=4, replica_groups=mesh['exp'=64,'sub'=4] {'exp'}, use_global_device_ids=true, to_apply=%region_3.4.clone | all-reduce | flops 512 | bytes 4096
  393.5 0.7 fusion.81
  394.2 1.4 fusion.86
  395.7 72.7 %all-gather.6.cloned.1.call-done = bf16[512,1024]{1,0:T(8,128)(2,1)} async-done(((bf16[8,1024]{1,0:T(8,128)(2,1)}), bf16[512,1024]{1,0:T(8,128)(2,1)}) %all-gather.6.cloned.1.call-update) | async-done | bytes 1048592 | tf_op jit(solution)/shard_map/all_gather | solution.py:74
  468.5 1.6 fusion.36
  470.1 3.4 collective-permute-start.4
  473.5 2.4 collective-permute-start.5
  476.0 3.3 collective-permute-done.5
  479.3 2.1 convert_bitcast_fusion
  481.5 1.9 fusion.40
  483.4 3.3 fusion.6
  486.7 6.6 copy.100
  493.3 4.1 fusion.2
  497.4 0.1 subtract_clamp_fusion
  497.5 0.8 copy-done.10
  498.3 2.4 fusion.3
  500.7 3.8 reshape.126
  504.5 3.3 fusion.21
  507.8 0.6 slice_bitcast_fusion.3
  508.5 0.4 copy-done.7
  508.9 1.2 fusion.28
  510.1 3.1 collective-permute-start.6
  513.2 2.8 collective-permute-start.7
  516.0 0.3 collective-permute-done.6
  516.3 3.1 collective-permute-done.7
  519.4 0.1 fusion.50
  519.4 2.4 fusion.44
  521.9 186.4 %all-reduce.22.cloned.1.call-done = f32[512,1024]{1,0:T(8,128)} async-done(((f32[512,1024]{1,0:T(8,128)}), f32[512,1024]{1,0:T(8,128)}) %all-reduce.22.cloned.1.call-update) | async-done | bytes 2097168
  708.3 0.9 fusion.76
  709.2 0.6 copy.108
  (44 shorter events, 0.6 us)
Async XLA Ops:
  7.2 3.3 copy-start
  7.2 83.8 %all-gather.4.cloned.1.call-start = ((), (), s32[]{:S(2)}) async-start(), calls=%async_computation | async-start | bytes 1064960 | tf_op jit(solution)/shard_map/all_gather | solution.py:74
  8.6 385.5 %all-reduce.20.cloned.1.call-start = ((), (), s32[]{:S(2)}) async-start(), calls=%async_computation.2 | async-start | bytes 4194304
  11.0 91.9 %copy-start.5 = (bf16[128,148,12]{0,2,1:T(8,128)(2,1)}, bf16[128,148,12]{0,2,1:T(8,128)(2,1)S(1)}, u32[]{:S(2)}) copy-start(bf16[128,148,12]{0,2,1:T(8,128)(2,1)S(1)} %fusion.26) | copy-start | bytes 1363972
  92.7 7.0 collective-permute-start
  96.1 5.8 collective-permute-start.1
  99.7 5.1 copy-start.3
  108.2 6.7 copy-start.2
  114.9 4.1 copy-start.8
  131.4 1.1 copy-start.6
  133.7 12.1 %copy-start.12 = (u32[256]{0:T(256)S(1)}, u32[256]{0:T(256)}, u32[]{:S(2)}) copy-start(u32[256]{0:T(256)} %constant.52) | copy-start | bytes 3076
  133.7 260.5 %copy-start.11 = (f32[1,8,8,128]{3,2,1,0:T(8,128)S(1)}, f32[1,8,8,128]{3,2,1,0:T(8,128)}, u32[]{:S(2)}) copy-start(f32[1,8,8,128]{3,2,1,0:T(8,128)} %param.7) | copy-start | bytes 98308
  133.7 6.2 collective-permute-start.2
  136.8 6.2 collective-permute-start.3
  145.5 323.0 %all-gather.6.cloned.1.call-start = ((), (), s32[]{:S(2)}) async-start(), calls=%async_computation.1 | async-start | bytes 1064960 | tf_op jit(solution)/shard_map/all_gather | solution.py:74
  395.7 312.6 %all-reduce.22.cloned.1.call-start = ((), (), s32[]{:S(2)}) async-start(), calls=%async_computation.3 | async-start | bytes 4194304
  470.1 5.9 collective-permute-start.4
  473.5 5.8 collective-permute-start.5
  481.5 1.9 copy-start.4
  493.3 4.1 copy-start.9
  497.5 0.8 copy-start.10
  507.8 1.1 copy-start.7
  508.9 200.9 %copy-start.1 = (bf16[12,21]{1,0:T(8,128)(2,1)S(1)}, bf16[12,21]{1,0:T(8,128)(2,1)}, u32[]{:S(2)}) copy-start(bf16[12,21]{1,0:T(8,128)(2,1)} %param.10) | copy-start | bytes 1516
  510.1 6.2 collective-permute-start.6
  513.2 6.2 collective-permute-start.7
Sparse Core Ops, SparseCore 0:
  11.3 79.6 all-gather.3
  145.6 186.6 all-reduce.19
  395.8 72.6 all-gather.5
  522.0 186.2 all-reduce.21
where the time goes:
time: 718 us; the launch traced here: 716 us
  waiting for transfers between devices  351 us (49%)
  blocking collectives  246 us (34%)
  local copies, waits for them, and re-layouts  32.5 us (5%)
  matrix products  29.4 us (4%)
  starting transfers between devices  23.7 us (3%)
  other arithmetic  18 us (3%)
  between operations  14.9 us (2%)
    unnamed x1, blocking collectives  246 us
    unnamed x6, waiting for transfers between devices  187 us
    all_gather x2, waiting for transfers between devices, per_device(): lax.all_gather(current.astype(jnp.bfloat16).reshape(1, per_tile, patch_si...  153 us
  transfers between devices with their start and end apart: 12, of which 9 were waited for; matrix products, arithmetic and copies ran while one was open for 1% of the time, Pallas kernels for 0%

commit v1 on v0

--- a/solution.py
+++ b/solution.py
@@ -71,8 +71,17 @@
     current = sky_map.reshape(per_tile, patch_size)
     clipped = jnp.zeros(observed.shape, jnp.float32)
     for step_index in range(STEPS):
-        shard_piece = lax.all_gather(
-            current.astype(jnp.bfloat16).reshape(1, per_tile, patch_size), "exp", axis=0, tiled=True
+        shard_piece = jnp.concatenate(
+            lax.all_to_all(
+                jnp.stack(
+                    [current.astype(jnp.bfloat16).reshape(1, per_tile, patch_size)]
+                    * lax.axis_size("exp")
+                ),
+                "exp",
+                0,
+                0,
+            ),
+            axis=0,
         )
         tile_count = shard_piece.shape[0]
         patches = jnp.dot(

time: 718 us -> 630 us (0.88)
  waiting for transfers between devices: 351 us -> 225 us
  blocking collectives: 246 us -> 279 us
  starting transfers between devices: 23.7 us -> 35.6 us
    all_gather x2 -> x0, waiting for transfers between devices: 153 us -> none  [per_device(): lax.all_gather(current.astype(jnp.bfloat16).reshape(1, per_tile, patch_si...]
    all_to_all x0 -> x1, blocking collectives: none -> 32.9 us  [per_device(): lax.all_to_all(jnp.stack([current.astype(jnp.bfloat16).reshape(1, per_til...]
    all_to_all x0 -> x1, waiting for transfers between devices: none -> 27.8 us  [per_device(): lax.all_to_all(jnp.stack([current.astype(jnp.bfloat16).reshape(1, per_til...]
    all_to_all x0 -> x1, starting transfers between devices: none -> 11.9 us  [per_device(): lax.all_to_all(jnp.stack([current.astype(jnp.bfloat16).reshape(1, per_til...]
    unnamed x6 -> x4, waiting for transfers between devices: 187 us -> 186 us
  transfers between devices with their start and end apart: 12 -> 11, of which waited for: 9 -> 8; matrix products, arithmetic and copies ran while one was open for 1% -> 0% of each run, Pallas kernels for 0% -> 0%
where the time goes in v1:
time: 630 us; the launch traced here: 629 us
  blocking collectives  279 us (44%)
  waiting for transfers between devices  225 us (36%)
  starting transfers between devices  35.6 us (6%)
  local copies, waits for them, and re-layouts  33.2 us (5%)
  matrix products  25.2 us (4%)
  other arithmetic  16 us (3%)
  between operations  15.2 us (2%)
    unnamed x1, blocking collectives  247 us
    unnamed x4, waiting for transfers between devices  186 us
    all_to_all x1, blocking collectives, per_device(): lax.all_to_all(jnp.stack([current.astype(jnp.bfloat16).reshape(1, per_til...  32.9 us
    all_to_all x1, waiting for transfers between devices, per_device(): lax.all_to_all(jnp.stack([current.astype(jnp.bfloat16).reshape(1, per_til...  27.8 us
    reshape x2, local copies, waits for them, and re-layouts, per_device(): blurred = jnp.einsum('pmbkw,mwc->pmbkc', windows, horizontal, preferred_e...  13.3 us
  transfers between devices with their start and end apart: 11, of which 8 were waited for; matrix products, arithmetic and copies ran while one was open for 0% of the time, Pallas kernels for 0%

profile of v1, /device:TPU:8, one launch (start us, length us, event | category | flops | bytes accessed | tf_op | source)
XLA Modules:
  0.0 629.2 jit_solution(18425456490402939336)
XLA Ops:
  7.2 0.8 copy.188
  8.0 1.1 stack.36
  9.1 11.9 %all-to-all-start = ((bf16[64,1,8,1024]{3,2,1,0:T(8,128)(2,1)}), bf16[64,1,8,1024]{3,2,1,0:T(8,128)(2,1)S(1)}, u32[]{:S(2)}, u32[]{:S(2)}) async-start(bf16[64,1,8,1024]{3,2,1,0:T(8,128)(2,1)} %stack.36), calls=%async_computation | async-start | bytes 2097152 | tf_op jit(solution)/shard_map/all_to_all | solution.py:75
  21.1 0.1 copy.84
  21.2 0.1 mul.53
  21.3 0.1 copy.85
  21.4 0.1 reshape.101
  21.6 0.5 fusion.26
  22.1 27.8 %all-to-all-done = bf16[64,1,8,1024]{3,2,1,0:T(8,128)(2,1)S(1)} async-done(((bf16[64,1,8,1024]{3,2,1,0:T(8,128)(2,1)}), bf16[64,1,8,1024]{3,2,1,0:T(8,128)(2,1)S(1)}, u32[]{:S(2)}, u32[]{:S(2)}) %all-to-all-start) | async-done | bytes 1048608 | tf_op jit(solution)/shard_map/all_to_all | solution.py:75
  49.9 0.4 fusion.35
  50.3 3.5 collective-permute-start
  53.8 2.4 collective-permute-start.1
  56.2 0.5 fusion.34
  56.7 2.9 collective-permute-done.1
  59.6 1.0 convert_bitcast_fusion.1
  60.7 1.9 fusion.39
  62.6 3.3 fusion.8
  65.9 6.7 %copy.89 = f32[2,12,128,512]{3,2,1,0:T(8,128)} copy(f32[2,12,128,512]{2,3,0,1:T(8,128)} %bitcast.160) | data formatting | bytes 12582912 | tf_op jit(solution)/shard_map/reshape | solution.py:114
  72.7 4.1 fusion
  76.8 0.1 subtract_clamp_fusion.1
  76.9 2.4 fusion.1
  79.3 5.5 reshape.105
  84.9 4.3 fusion.18
  89.2 0.6 slice_bitcast_fusion.7
  89.8 0.4 copy-done.6
  90.2 1.2 fusion.31
  91.5 3.2 collective-permute-start.2
  94.7 2.8 collective-permute-start.3
  97.5 0.1 collective-permute-done.2
  97.6 3.2 collective-permute-done.3
  100.9 2.4 fusion.48
  103.4 0.1 convert_reduce_fusion
  103.5 0.1 reshape.108
  103.7 0.6 dynamic-slice
  104.9 246.5 %all-reduce.15 = f32[64,8]{1,0:T(8,128)S(1)} all-reduce(f32[64,8]{1,0:T(8,128)S(1)} %reshape.108), channel_id=3, replica_groups=mesh['exp'=64,'sub'=4] {'exp'}, use_global_device_ids=true, to_apply=%region_3.4.clone | all-reduce | flops 512 | bytes 4096
  351.4 0.7 fusion.82
  352.1 0.9 fusion.87
  353.0 0.1 stack.42
  353.1 32.9 %all_to_all.10 = bf16[64,1,8,1024]{3,2,1,0:T(8,128)(2,1)S(1)} all-to-all(bf16[64,1,8,1024]{3,2,1,0:T(8,128)(2,1)S(1)} %stack.42), channel_id=1, replica_groups=mesh['exp'=64,'sub'=4] {'exp'}, dimensions={0} | all-to-all | bytes 2097152 | tf_op jit(solution)/shard_map/all_to_all | solution.py:75
  386.1 0.3 fusion.36
  386.5 2.1 collective-permute-start.4
  388.6 3.7 collective-permute-start.5
  392.4 2.1 collective-permute-done.5
  394.4 1.0 convert_bitcast_fusion
  395.5 1.9 fusion.41
  397.4 3.3 fusion.6
  400.7 6.6 %copy.100 = f32[2,12,128,512]{3,2,1,0:T(8,128)} copy(f32[2,12,128,512]{2,3,0,1:T(8,128)} %bitcast.161) | data formatting | bytes 12582912 | tf_op jit(solution)/shard_map/reshape | solution.py:114
  407.3 4.1 fusion.2
  411.4 0.1 subtract_clamp_fusion
  411.6 0.8 copy-done.11
  412.3 2.4 fusion.3
  414.8 3.8 reshape.112
  418.5 3.3 fusion.21
  421.8 0.6 slice_bitcast_fusion.3
  422.5 0.4 copy-done.8
  422.9 1.2 fusion.28
  424.1 1.9 collective-permute-start.6
  426.1 3.9 collective-permute-start.7
  430.0 0.3 collective-permute-done.6
  430.3 1.9 collective-permute-done.7
  432.3 2.4 fusion.45
  434.7 186.2 %all-reduce.22.cloned.1.call-done = f32[512,1024]{1,0:T(8,128)} async-done(((f32[512,1024]{1,0:T(8,128)}), f32[512,1024]{1,0:T(8,128)}) %all-reduce.22.cloned.1.call-update) | async-done | bytes 2097168
  620.9 0.9 fusion.77
  621.8 0.6 copy.108
  (50 shorter events, 0.5 us)
Async XLA Ops:
  7.2 14.4 %copy-start = (bf16[12,21]{1,0:T(8,128)(2,1)S(1)}, bf16[12,21]{1,0:T(8,128)(2,1)}, u32[]{:S(2)}) copy-start(bf16[12,21]{1,0:T(8,128)(2,1)} %param.10) | copy-start | bytes 1516
  7.2 13.9 %copy-start.15 = (s32[2,16,4,1]{1,3,2,0:T(1,128)S(1)}, s32[2,16,4,1]{1,3,2,0:T(1,128)}, u32[]{:S(2)}) copy-start(s32[2,16,4,1]{1,3,2,0:T(1,128)} %param.12) | copy-start | bytes 1540
  7.2 14.1 %copy-start.14 = (s32[2,16,4]{1,2,0:T(4,128)S(1)}, s32[2,16,4]{1,2,0:T(4,128)}, u32[]{:S(2)}) copy-start(s32[2,16,4]{1,2,0:T(4,128)} %param.13) | copy-start | bytes 1540
  7.2 49.0 %copy-start.13 = (bf16[12,21]{1,0:T(8,128)(2,1)S(1)}, bf16[12,21]{1,0:T(8,128)(2,1)}, u32[]{:S(2)}) copy-start(bf16[12,21]{1,0:T(8,128)(2,1)} %param.11) | copy-start | bytes 1516
  9.1 40.8 %all-to-all-start = ((bf16[64,1,8,1024]{3,2,1,0:T(8,128)(2,1)}), bf16[64,1,8,1024]{3,2,1,0:T(8,128)(2,1)S(1)}, u32[]{:S(2)}, u32[]{:S(2)}) async-start(bf16[64,1,8,1024]{3,2,1,0:T(8,128)(2,1)} %stack.36), calls=%async_computation | async-start | bytes 2097152 | tf_op jit(solution)/shard_map/all_to_all | solution.py:75
  21.1 331.0 %all-reduce.20.cloned.1.call-start = ((), (), s32[]{:S(2)}) async-start(), calls=%async_computation.2 | async-start | bytes 4194304
  22.1 38.6 %copy-start.5 = (bf16[128,148,12]{0,2,1:T(8,128)(2,1)}, bf16[128,148,12]{0,2,1:T(8,128)(2,1)S(1)}, u32[]{:S(2)}) copy-start(bf16[128,148,12]{0,2,1:T(8,128)(2,1)S(1)} %fusion.26) | copy-start | bytes 1363972
  50.3 6.4 %collective-permute-start = (bf16[2,10,512]{2,1,0:T(8,128)(2,1)S(1)}, bf16[2,10,512]{2,1,0:T(8,128)(2,1)S(1)}, u32[]{:S(2)}, u32[]{:S(2)}) collective-permute-start(bf16[2,10,512]{2,1,0:T(8,128)(2,1)S(1)} %get-tuple-element.32), channel_id=1, source_target_pairs={{0,1},{1,2},{2,3},{4,5},{5,6},{6,7},{8,9},{9,10},{10,11},{12,13},{... | collective-permute-start | bytes 61448 | tf_op jit(solution)/shard_map/ppermute | solution.py:19
  53.8 5.8 collective-permute-start.1
  56.7 5.9 copy-start.3
  65.9 6.7 %copy-start.2 = (bf16[2,12,128,512]{3,2,1,0:T(8,128)(2,1)S(1)}, bf16[2,12,128,512]{3,2,1,0:T(8,128)(2,1)}, u32[]{:S(2)}) copy-start(bf16[2,12,128,512]{3,2,1,0:T(8,128)(2,1)} %param.8) | copy-start | bytes 9437188
  72.7 4.1 copy-start.9
  89.2 1.1 copy-start.6
  91.4 12.2 %copy-start.16 = (u32[256]{0:T(256)S(1)}, u32[256]{0:T(256)}, u32[]{:S(2)}) copy-start(u32[256]{0:T(256)} %constant.52) | copy-start | bytes 3076
  91.4 260.6 %copy-start.12 = (f32[1,8,8,128]{3,2,1,0:T(8,128)S(1)}, f32[1,8,8,128]{3,2,1,0:T(8,128)}, u32[]{:S(2)}) copy-start(f32[1,8,8,128]{3,2,1,0:T(8,128)} %param.7) | copy-start | bytes 98308
  91.5 6.2 collective-permute-start.2
  94.7 6.2 collective-permute-start.3
  103.4 517.5 %all-reduce.22.cloned.1.call-start = ((), (), s32[]{:S(2)}) async-start(), calls=%async_computation.3 | async-start | bytes 4194304
  352.1 42.3 %copy-start.7 = (bf16[128,148,12]{0,2,1:T(8,128)(2,1)S(1)}, bf16[128,148,12]{0,2,1:T(8,128)(2,1)}, u32[]{:S(2)}) copy-start(bf16[128,148,12]{0,2,1:T(8,128)(2,1)} %copy-done.5) | copy-start | bytes 1363972
  386.5 5.9 collective-permute-start.4
  388.6 5.8 collective-permute-start.5
  395.5 1.9 copy-start.4
  407.3 4.1 copy-start.10
  411.5 0.8 copy-start.11
  421.8 1.1 copy-start.8
  422.9 199.5 %copy-start.1 = (bf16[12,21]{1,0:T(8,128)(2,1)S(1)}, bf16[12,21]{1,0:T(8,128)(2,1)}, u32[]{:S(2)}) copy-start(bf16[12,21]{1,0:T(8,128)(2,1)} %param.10) | copy-start | bytes 1516
  424.1 6.2 collective-permute-start.6
  426.1 6.2 collective-permute-start.7
Sparse Core Ops, SparseCore 0:
  103.5 186.5 all-reduce.19
  434.8 186.0 all-reduce.21
